TPU v7x, 32 devices: a whole 2x2x4 slice. The times are simulated.
32 devices in a mesh: dp: 16 (over z, x, core), fsdp: 2 (over y).
Axes of the slice: x: 2, y: 2, z: 4, core: 2. Of those that a mesh axis runs over, the one named last changes fastest.
Arguments:
- waveform: float32 [256, 400], P(('dp', 'fsdp')), may hold values from -6 to 6
- lengths: int32 [256], P(('dp', 'fsdp')), may hold values from 200 to 400, as said below
- owner_of: int32 [256], P(('dp', 'fsdp')), may hold values from 0 to 15, as said below
- targets: float32 [256, 39], P(('dp', 'fsdp')), may hold values from -5 to 5
- first_weight: float32 [10, 512], replicated, may hold values from -2 to 2
- first_gain: float32 [512], replicated, may hold values from 0.1 to 1.9
- first_shift: float32 [512], replicated, may hold values from -3 to 3
- second_weight: bfloat16 [1536, 512], P('fsdp'), may hold values from -0.15625 to 0.15625
- second_gain: float32 [512], replicated, may hold values from 0.1 to 1.9
- second_shift: float32 [512], replicated, may hold values from -3 to 3
Outputs:
- logvar: float32 [256, 39], P(('dp', 'fsdp'))
- loss: float32 [], replicated
- grad_second_weight: float32 [1536, 512], P('fsdp')
- grad_first_weight: float32 [10, 512], replicated
- grad_first_gain: float32 [512], replicated
- grad_first_shift: float32 [512], replicated
- grad_second_gain: float32 [512], replicated
- grad_second_shift: float32 [512], replicated
Inputs may be any that keep to these rules, and one draw needn't show every extreme that they name: `lengths`: every draw has a row of length 400 and one of length 200. `owner_of`: rows read by the devices of one fsdp index go to owners of the same fsdp index. From one reader, each owner receives either no row or exactly 1 row; every owner receives exactly 8 rows.
All inputs are finite; a program needn't handle non-finite values.
Results may differ from a plain program's by a relative error of at most 0.0019.
Values may be sent and summed in bfloat16 or wider, within the bound.
No kernel may reach another device: no remote copies, remote signals or barrier semaphores. Data moves between devices by JAX's collectives and lax.ppermute only.
A program may use at most 64 MiB of HBM per device.

v0:
```python
import jax
import jax.numpy as jnp
from jax import lax
from jax.sharding import PartitionSpec as P

epsilon = 1e-05


def layer_norm(values, norm_gain, norm_shift):
    row_mean = jnp.mean(values, axis=-1, keepdims=True)
    centered = values - row_mean
    row_var = jnp.mean(centered * centered, axis=-1, keepdims=True)
    return centered * lax.rsqrt(row_var + epsilon) * norm_gain + norm_shift


def first_layer(waveform, first_weight, first_gain, first_shift):
    row_total, samples = waveform.shape
    frames = samples // 5 - 1
    blocks = waveform.reshape(row_total, samples // 5, 5)
    windows = jnp.concatenate([blocks[:, :frames], blocks[:, 1 : frames + 1]], axis=2)
    pre_norm = jnp.dot(
        windows.reshape(row_total * frames, 10),
        first_weight,
        precision=lax.Precision.HIGHEST,
        preferred_element_type=jnp.float32,
    )
    return jax.nn.gelu(layer_norm(pre_norm, first_gain, first_shift), approximate=False)


def make_patches(activated, row_total):
    channels = activated.shape[1]
    frames = activated.shape[0] // row_total
    later = (frames - 1) // 2
    shaped = activated.reshape(row_total, frames, channels)
    padded = jnp.concatenate([shaped, jnp.zeros((row_total, 1, channels), activated.dtype)], axis=1)
    paired = padded.reshape(row_total, later + 1, 2, channels)
    even_frames = paired[:, :, 0]
    odd_frames = paired[:, :, 1]
    joined = jnp.concatenate(
        [even_frames[:, :later], odd_frames[:, :later], even_frames[:, 1:]], axis=2
    )
    return joined.reshape(row_total * later, 3 * channels)


def patch_grad(grad_patches, row_total, frames):
    channels = grad_patches.shape[1] // 3
    later = grad_patches.shape[0] // row_total
    shaped = grad_patches.reshape(row_total, later, 3, channels)
    zero_frame = jnp.zeros((row_total, 1, channels), grad_patches.dtype)
    even_frames = jnp.concatenate([shaped[:, :, 0], zero_frame], axis=1) + jnp.concatenate(
        [zero_frame, shaped[:, :, 2]], axis=1
    )
    odd_frames = jnp.concatenate([shaped[:, :, 1], zero_frame], axis=1)
    paired = jnp.stack([even_frames, odd_frames], axis=2).reshape(
        row_total, 2 * later + 2, channels
    )
    return paired[:, :frames].reshape(row_total * frames, channels)


def frame_mask_of(row_lengths, later):
    first_valid = (row_lengths - 10) // 5 + 1
    second_valid = (first_valid - 3) // 2 + 1
    inside = jnp.arange(later, dtype=jnp.int32)[None, :] < second_valid[:, None]
    return inside.astype(jnp.float32).reshape(-1)


def head_loss(second_pre, second_gain, second_shift, target_flat, frame_mask):
    activated = jax.nn.gelu(layer_norm(second_pre, second_gain, second_shift), approximate=False)
    row_mean = jnp.mean(activated, axis=-1, keepdims=True)
    centered = activated - row_mean
    raw_logvar = jnp.log(jnp.mean(centered * centered, axis=-1) + epsilon)
    misfit = raw_logvar - target_flat
    return (jnp.sum(frame_mask * misfit * misfit), raw_logvar)


def per_device(
    waveform,
    lengths,
    owner_of,
    targets,
    first_weight,
    first_gain,
    first_shift,
    second_weight,
    second_gain,
    second_shift,
):
    peer_count = lax.axis_size("dp")
    row_total, samples = waveform.shape
    later = targets.shape[1]
    frames = samples // 5 - 1
    per_owner = max(1, 2 * row_total // peer_count)
    slot_count = peer_count * per_owner
    matches = (owner_of[:, None] == owner_of[None, :]).astype(jnp.int32)
    earlier = jnp.sum(jnp.tril(matches, -1), axis=1)
    slot_index = owner_of * per_owner + earlier
    placing = (slot_index[:, None] == jnp.arange(slot_count, dtype=jnp.int32)[None, :]).astype(
        jnp.float32
    )
    sent_wave = lax.dot_general(
        placing,
        waveform,
        (((0,), (0,)), ((), ())),
        precision=lax.Precision.HIGHEST,
        preferred_element_type=jnp.float32,
    )
    sent_length = jnp.dot(
        lengths.astype(jnp.float32),
        placing,
        precision=lax.Precision.HIGHEST,
        preferred_element_type=jnp.float32,
    )
    got_wave, got_length = (
        lax.all_to_all(
            sent_wave.reshape(peer_count, per_owner, samples),
            "dp",
            split_axis=0,
            concat_axis=0,
            tiled=True,
        ),
        lax.all_to_all(
            sent_length.reshape(peer_count, per_owner),
            "dp",
            split_axis=0,
            concat_axis=0,
            tiled=True,
        ),
    )
    got_wave = got_wave.reshape(slot_count, samples)
    got_length = got_length.reshape(slot_count)
    present = got_length > 0.5
    arrival = jnp.cumsum(present.astype(jnp.int32)) - 1
    picking = (
        present[None, :] & (arrival[None, :] == jnp.arange(row_total, dtype=jnp.int32)[:, None])
    ).astype(jnp.float32)
    owned_wave = jnp.dot(
        picking, got_wave, precision=lax.Precision.HIGHEST, preferred_element_type=jnp.float32
    )
    owned_length = jnp.dot(
        picking, got_length, precision=lax.Precision.HIGHEST, preferred_element_type=jnp.float32
    ).astype(jnp.int32)

    def first_part(weight_first, gain_first, shift_first):
        return first_layer(owned_wave, weight_first, gain_first, shift_first)

    activated, first_pull = jax.vjp(first_part, first_weight, first_gain, first_shift)
    rounded = activated.astype(jnp.bfloat16)
    patches = make_patches(rounded, row_total)
    columns = patches
    second_pre = jnp.dot(
        columns,
        lax.all_gather(second_weight, "fsdp", axis=0, tiled=True),
        preferred_element_type=jnp.float32,
    )
    frame_mask = frame_mask_of(owned_length, later)

    def head_part(pre_norm, gain_second, shift_second):
        return head_loss(pre_norm, gain_second, shift_second, targets.reshape(-1), frame_mask)

    loss_sum, head_pull, raw_logvar = jax.vjp(
        head_part, second_pre, second_gain, second_shift, has_aux=True
    )
    grad_pre, grad_gain_two, grad_shift_two = head_pull(jnp.ones_like(loss_sum))
    grad_pre = grad_pre.astype(jnp.bfloat16)
    columns = patches
    grad_shard = lax.psum_scatter(
        lax.dot_general(
            columns, grad_pre, (((0,), (0,)), ((), ())), preferred_element_type=jnp.float32
        ).astype(jnp.bfloat16),
        "fsdp",
        scatter_dimension=0,
        tiled=True,
    ).astype(jnp.float32)
    grad_weight_two = lax.psum(grad_shard, "dp")
    grad_patches = lax.dot_general(
        grad_pre,
        lax.all_gather(second_weight, "fsdp", axis=0, tiled=True),
        (((1,), (1,)), ((), ())),
        preferred_element_type=jnp.float32,
    )
    grad_act = patch_grad(grad_patches, row_total, frames)
    grad_weight_one, grad_gain_one, grad_shift_one = first_pull(grad_act)
    summed = lax.psum(
        (
            grad_weight_one,
            grad_gain_one,
            grad_shift_one,
            grad_gain_two,
            grad_shift_two,
            loss_sum,
            jnp.sum(frame_mask),
        ),
        ("dp", "fsdp"),
    )
    logvar = (raw_logvar * frame_mask).reshape(row_total, later)
    loss = summed[5] / summed[6]
    return (logvar, loss, grad_weight_two, summed[0], summed[1], summed[2], summed[3], summed[4])


def solution(mesh):
    placed = (
        P(("dp", "fsdp"), None),
        P(("dp", "fsdp")),
        P(("dp", "fsdp")),
        P(("dp", "fsdp"), None),
        P(),
        P(),
        P(),
        P("fsdp", None),
        P(),
        P(),
    )
    return jax.shard_map(
        per_device,
        mesh=mesh,
        in_specs=placed,
        out_specs=(P(("dp", "fsdp"), None), P(), P("fsdp", None), P(), P(), P(), P(), P()),
        check_vma=False,
    )
```

profile of v0, /device:TPU:0, one launch (start us, length us, event | category | flops | bytes accessed | tf_op | source)
XLA Modules:
  0.0 200.0 jit_solution(7417395136879654368)
XLA Ops:
  7.2 0.9 select_reduce_fusion
  8.8 1.5 fusion.21
  10.3 7.4 %all-to-all-start = ((f32[16,1,1]{2,1,0:T(1,128)}), f32[16,1,1]{2,1,0:T(1,128)S(1)}, u32[]{:S(2)}, u32[]{:S(2)}) async-start(f32[16,1,1]{2,1,0:T(1,128)} %bitcast.21), calls=%async_computation | async-start | bytes 16384 | tf_op jit(solution)/shard_map/all_to_all | solution.py:121
  18.4 1.0 convolution_bitcast_fusion
  20.8 3.2 %all-to-all-done = f32[16,1,1]{2,1,0:T(1,128)S(1)} async-done(((f32[16,1,1]{2,1,0:T(1,128)}), f32[16,1,1]{2,1,0:T(1,128)S(1)}, u32[]{:S(2)}, u32[]{:S(2)}) %all-to-all-start) | async-done | bytes 96 | tf_op jit(solution)/shard_map/all_to_all | solution.py:121
  24.0 3.5 %all-to-all-start.1 = ((f32[16,1,400]{2,1,0:T(1,128)}), f32[16,1,400]{2,1,0:T(1,128)S(1)}, u32[]{:S(2)}, u32[]{:S(2)}) async-start(f32[16,1,400]{2,1,0:T(1,128)} %copy.79), calls=%async_computation.1 | async-start | bytes 65536 | tf_op jit(solution)/shard_map/all_to_all | solution.py:114
  28.3 5.8 %all-to-all-done.1 = f32[16,1,400]{2,1,0:T(1,128)S(1)} async-done(((f32[16,1,400]{2,1,0:T(1,128)}), f32[16,1,400]{2,1,0:T(1,128)S(1)}, u32[]{:S(2)}, u32[]{:S(2)}) %all-to-all-start.1) | async-done | bytes 25632 | tf_op jit(solution)/shard_map/all_to_all | solution.py:114
  34.9 1.3 fusion.55
  36.5 4.4 %multiply_convert_fusion = (bf16[632,512]{1,0:T(8,128)(2,1)S(1)}, f32[632,512]{1,0:T(8,128)}) fusion(f32[632,512]{1,0:T(8,128)S(1)} %get-tuple-element.47, f32[512]{0:T(512)S(1)} %copy-done.6, f32[512]{0:T(512)S(1)} %copy-done.2, f32[632]{0:T(1024)S(1)} %fusion.26, f32[632]{0:T(1024)S(1)} %broadcast_multiply_fusion), kind=kLoop, calls=%fused_computation.10 | loop fusion | flops 22327296 | bytes 3244992 | tf_op jit(solution)/shard_map/convert_element_type | solution.py:147
  41.4 1.2 fusion.52
  43.3 5.4 %all-gather.2.cloned.1.call-done = bf16[1536,512]{1,0:T(8,128)(2,1)} async-done(((bf16[768,512]{1,0:T(8,128)(2,1)}), bf16[1536,512]{1,0:T(8,128)(2,1)}) %all-gather.2.cloned.1.call-update) | async-done | bytes 1572880 | tf_op jit(solution)/shard_map/all_gather | solution.py:152
  48.6 2.2 %fusion.56 = (f32[312]{0:T(512)S(1)}, f32[312,512]{1,0:T(8,128)S(1)}) fusion(bf16[312,1536]{1,0:T(8,128)(2,1)S(1)} %reshape.195, bf16[1536,512]{1,0:T(8,128)(2,1)} %all-gather.2.cloned.1.call-done), kind=kOutput, calls=%fused_computation.124 | convolution fusion | flops 490892992 | bytes 3171552 | tf_op jit(solution)/shard_map/dot_general | solution.py:150
  51.1 1.7 fusion.48
  54.4 0.8 copy-done.1
  55.3 2.2 %convolution_convert_fusion = bf16[1536,512]{1,0:T(8,128)(2,1)} fusion(bf16[312,1536]{1,0:T(8,128)(2,1)S(1)} %reshape.195, f32[312,512]{1,0:T(8,128)S(1)} %get-tuple-element.27, f32[312]{0:T(512)S(1)} %negate_multiply_fusion.3), kind=kOutput, calls=%fused_computation | convolution fusion | flops 491839488 | bytes 3171552 | tf_op jit(solution)/shard_map/dot_general | solution.py:167
  57.5 2.3 %fusion.45 = f32[312,1536]{1,0:T(8,128)S(1)} fusion(bf16[1536,512]{1,0:T(8,128)(2,1)} %all-gather.2.cloned.1.call-done, f32[312,512]{1,0:T(8,128)} %copy-done.1, f32[312]{0:T(512)S(1)} %negate_multiply_fusion.3), kind=kOutput, calls=%fused_computation.115 | convolution fusion | flops 491053056 | bytes 4130016 | tf_op jit(solution)/shard_map/dot_general | solution.py:175
  59.8 2.7 %reshape.197 = f32[8,39,3,512]{3,2,1,0:T(4,128)} reshape(f32[312,1536]{1,0:T(8,128)S(1)} %fusion.45) | data formatting | bytes 3833856 | tf_op jit(solution)/shard_map/reshape | solution.py:48
  62.6 5.6 %fusion.51 = (f32[8,39,1,512]{3,2,1,0:T(1,128)S(1)}, f32[8,39,1,512]{3,2,1,0:T(1,128)S(1)}, f32[8,39,1,512]{3,2,1,0:T(1,128)S(1)}) fusion(f32[8,39,3,512]{3,2,1,0:T(4,128)} %reshape.197), kind=kLoop, calls=%fused_computation.119 | loop fusion | bytes 3833856 | tf_op jit(solution)/shard_map/slice | solution.py:50
  69.6 1.2 reshape.199
  70.9 2.9 %multiply_reduce_fusion = (f32[512]{0:T(512)S(1)}, f32[632]{0:T(1024)S(1)}, f32[512]{0:T(512)S(1)}, f32[632,512]{1,0:T(8,128)S(1)}) fusion(f32[632,512]{1,0:T(8,128)S(1)} %get-tuple-element.47, f32[632]{0:T(1024)S(1)} %fusion.26, f32[632]{0:T(1024)S(1)} %broadcast_multiply_fusion, f32[512]{0:T(512)S(1)} %copy-done.2, f32[632,512]{1,0:T(8,128)} %reshape.199, ...), kind=kLoop, calls=%fused_computation.5 | loop fusion | flops 7440776 | bytes 5193120 | tf_op jit(solution)/shard_map/transpose(jvp())/reduce_sum | solution.py:13
  74.5 1.3 convert_reduce_fusion
  75.8 0.8 fusion.1
  76.7 40.4 %all-reduce.4 = (f32[]{:T(128)}, f32[]{:T(128)}, f32[10,512]{1,0:T(8,128)}, f32[512]{0:T(512)}, f32[512]{0:T(512)}, /*index=5*/f32[512]{0:T(512)}, f32[512]{0:T(512)}) all-reduce(f32[]{:T(128)} %get-tuple-element.15, f32[]{:T(128)} %get-tuple-element.14, f32[10,512]{1,0:T(8,128)S(1)} %fusion.1, ...), channel_id=1, replica_groups=mesh['dp'=16,'fsdp'=2] {'dp','fsdp'}, use_global_device_ids=true, to_apply=%region_9.10 | all-reduce | flops 7170 | bytes 57360 | tf_op jit(solution)/shard_map/psum | solution.py:183
  118.4 73.7 %all-reduce.6 = f32[768,512]{1,0:T(8,128)} all-reduce(bf16[768,512]{1,0:T(8,128)(2,1)} %reduce-scatter.2.cloned.1.call-done), channel_id=1, replica_groups=mesh['dp'=16,'fsdp'=2] {'dp'}, use_global_device_ids=true, to_apply=%region_16.17 | all-reduce | flops 393216 | bytes 2359296 | tf_op jit(solution)/shard_map/psum | solution.py:174
  (71 shorter events, 9.7 us)
Async XLA Ops:
  7.2 27.7 %copy-start = (f32[10,512]{1,0:T(8,128)S(1)}, f32[10,512]{1,0:T(8,128)}, u32[]{:S(2)}) copy-start(f32[10,512]{1,0:T(8,128)} %param.14) | copy-start | bytes 61444
  10.3 13.8 %all-to-all-start = ((f32[16,1,1]{2,1,0:T(1,128)}), f32[16,1,1]{2,1,0:T(1,128)S(1)}, u32[]{:S(2)}, u32[]{:S(2)}) async-start(f32[16,1,1]{2,1,0:T(1,128)} %bitcast.21), calls=%async_computation | async-start | bytes 16384 | tf_op jit(solution)/shard_map/all_to_all | solution.py:121
  17.7 31.0 %all-gather.2.cloned.1.call-start = ((), (), s32[]{:S(2)}) async-start(), calls=%async_computation.3 | async-start | bytes 2359296 | tf_op jit(solution)/shard_map/all_gather | solution.py:152
  24.0 10.1 %all-to-all-start.1 = ((f32[16,1,400]{2,1,0:T(1,128)}), f32[16,1,400]{2,1,0:T(1,128)S(1)}, u32[]{:S(2)}, u32[]{:S(2)}) async-start(f32[16,1,400]{2,1,0:T(1,128)} %copy.79), calls=%async_computation.1 | async-start | bytes 65536 | tf_op jit(solution)/shard_map/all_to_all | solution.py:114
  27.5 90.8 %reduce-scatter.2.cloned.1.call-start = ((), (), s32[]{:S(2)}) async-start(), calls=%async_computation.4 | async-start | bytes 2359296 | tf_op jit(solution)/shard_map/reduce_scatter | solution.py:166
  34.8 1.6 copy-start.2
  34.8 1.6 copy-start.6
  43.3 7.8 %copy-start.3 = (f32[512]{0:T(512)S(1)}, f32[512]{0:T(512)}, u32[]{:S(2)}) copy-start(f32[512]{0:T(512)} %param.18) | copy-start | bytes 6148
  43.3 7.8 %copy-start.5 = (f32[512]{0:T(512)S(1)}, f32[512]{0:T(512)}, u32[]{:S(2)}) copy-start(f32[512]{0:T(512)} %param.19) | copy-start | bytes 6148
  54.4 0.9 copy-start.1
  73.8 0.7 copy-start.4
Sparse Core Ops, SparseCore 0:
  20.0 28.5 all-gather.1
  57.6 26.1 reduce-scatter.1
where the time goes:
time: 201 us; the launch traced here: 200 us
  blocking collectives  114 us (57%)
  between operations  16.8 us (8%)
  local copies, waits for them, and re-layouts  15.8 us (8%)
  other arithmetic  15.4 us (8%)
  waiting for transfers between devices  15.2 us (8%)
  matrix products  11.8 us (6%)
  starting transfers between devices  11 us (5%)
    psum x1, blocking collectives, per_device(): grad_weight_two = lax.psum(grad_shard, 'dp')  73.7 us
    psum x1, blocking collectives, per_device(): lax.psum((grad_weight_one, grad_gain_one, grad_shift_one, grad_gain_two,...  40.4 us
    all_to_all x1, starting transfers between devices, per_device(): lax.all_to_all(sent_length.reshape(peer_count, per_owner), 'dp', split_ax...  7.39 us
    all_to_all x1, waiting for transfers between devices, per_device(): lax.all_to_all(sent_wave.reshape(peer_count, per_owner, samples), 'dp', s...  5.85 us
    slice x2, local copies, waits for them, and re-layouts, patch_grad(): shaped[:, :, 0]  5.62 us
    all_gather x1, waiting for transfers between devices, per_device(): lax.all_gather(second_weight, 'fsdp', axis=0, tiled=True)  5.37 us
    convert_element_type x1, other arithmetic, per_device(): rounded = activated.astype(jnp.bfloat16)  4.39 us
  transfers between devices with their start and end apart: 4, of which 3 were waited for; matrix products, arithmetic and copies ran while one was open for 15% of the time, Pallas kernels for 0%

commit v1 on v0

--- a/solution.py
+++ b/solution.py
@@ -171,7 +171,7 @@
         scatter_dimension=0,
         tiled=True,
     ).astype(jnp.float32)
-    grad_weight_two = lax.psum(grad_shard, "dp")
+    grad_weight_two = jnp.sum(lax.all_gather(grad_shard, "dp"), axis=0)
     grad_patches = lax.dot_general(
         grad_pre,
         lax.all_gather(second_weight, "fsdp", axis=0, tiled=True),

time: 201 us -> 228 us (1.13)
  waiting for transfers between devices: 15.2 us -> 99.9 us
  blocking collectives: 114 us -> 42.9 us
  other arithmetic: 15.4 us -> 28.8 us
    psum x1 -> x0, blocking collectives: 73.7 us -> none  [per_device(): grad_weight_two = lax.psum(grad_shard, 'dp')]
    all_gather x0 -> x1, waiting for transfers between devices: none -> 66 us  [per_device(): grad_weight_two = jnp.sum(lax.all_gather(grad_shard, 'dp'), axis=0)]
    reduce_scatter x1, waiting for transfers between devices: 0.02 us -> 23.4 us  [per_device(): lax.psum_scatter(lax.dot_general(columns, grad_pre, (((0,), (0,)), ((), (...]
    reduce_sum x0 -> x1, other arithmetic: none -> 10.9 us  [per_device(): grad_weight_two = jnp.sum(lax.all_gather(grad_shard, 'dp'), axis=0)]
    all_gather x1, waiting for transfers between devices: 5.37 us -> 0.02 us  [per_device(): lax.all_gather(second_weight, 'fsdp', axis=0, tiled=True)]
    all_gather x0 -> x1, other arithmetic: none -> 2.49 us  [per_device(): grad_weight_two = jnp.sum(lax.all_gather(grad_shard, 'dp'), axis=0)]
    psum x1, blocking collectives: 40.4 us -> 42.9 us  [per_device(): lax.psum((grad_weight_one, grad_gain_one, grad_shift_one, grad_gain_two,...]
  transfers between devices with their start and end apart: 4 -> 5, of which waited for: 3 -> 4; matrix products, arithmetic and copies ran while one was open for 15% -> 15% of each run, Pallas kernels for 0% -> 0%
where the time goes in v1:
time: 228 us; the launch traced here: 227 us
  waiting for transfers between devices  99.9 us (44%)
  blocking collectives  42.9 us (19%)
  other arithmetic  28.8 us (13%)
  between operations  16.5 us (7%)
  local copies, waits for them, and re-layouts  16.3 us (7%)
  matrix products  11.8 us (5%)
  starting transfers between devices  11.2 us (5%)
    all_gather x1, waiting for transfers between devices, per_device(): grad_weight_two = jnp.sum(lax.all_gather(grad_shard, 'dp'), axis=0)  66 us
    psum x1, blocking collectives, per_device(): lax.psum((grad_weight_one, grad_gain_one, grad_shift_one, grad_gain_two,...  42.9 us
    reduce_scatter x1, waiting for transfers between devices, per_device(): lax.psum_scatter(lax.dot_general(columns, grad_pre, (((0,), (0,)), ((), (...  23.4 us
    reduce_sum x1, other arithmetic, per_device(): grad_weight_two = jnp.sum(lax.all_gather(grad_shard, 'dp'), axis=0)  10.9 us
    all_to_all x1, starting transfers between devices, per_device(): lax.all_to_all(sent_length.reshape(peer_count, per_owner), 'dp', split_ax...  7.39 us
    slice x2, local copies, waits for them, and re-layouts, patch_grad(): shaped[:, :, 0]  6.15 us
    all_to_all x1, waiting for transfers between devices, per_device(): lax.all_to_all(sent_wave.reshape(peer_count, per_owner, samples), 'dp', s...  5.85 us
  transfers between devices with their start and end apart: 5, of which 4 were waited for; matrix products, arithmetic and copies ran while one was open for 15% of the time, Pallas kernels for 0%

profile of v1, /device:TPU:0, one launch (start us, length us, event | category | flops | bytes accessed | tf_op | source)
XLA Modules:
  0.0 227.4 jit_solution(13642651888016086005)
XLA Ops:
  7.9 0.9 select_reduce_fusion
  9.5 1.5 fusion.21
  11.0 7.4 %all-to-all-start = ((f32[16,1,1]{2,1,0:T(1,128)}), f32[16,1,1]{2,1,0:T(1,128)S(1)}, u32[]{:S(2)}, u32[]{:S(2)}) async-start(f32[16,1,1]{2,1,0:T(1,128)} %bitcast.22), calls=%async_computation | async-start | bytes 16384 | tf_op jit(solution)/shard_map/all_to_all | solution.py:121
  18.4 1.0 convolution_bitcast_fusion
  20.8 3.9 %all-to-all-done = f32[16,1,1]{2,1,0:T(1,128)S(1)} async-done(((f32[16,1,1]{2,1,0:T(1,128)}), f32[16,1,1]{2,1,0:T(1,128)S(1)}, u32[]{:S(2)}, u32[]{:S(2)}) %all-to-all-start) | async-done | bytes 96 | tf_op jit(solution)/shard_map/all_to_all | solution.py:121
  24.8 3.5 %all-to-all-start.1 = ((f32[16,1,400]{2,1,0:T(1,128)}), f32[16,1,400]{2,1,0:T(1,128)S(1)}, u32[]{:S(2)}, u32[]{:S(2)}) async-start(f32[16,1,400]{2,1,0:T(1,128)} %copy.79), calls=%async_computation.1 | async-start | bytes 65536 | tf_op jit(solution)/shard_map/all_to_all | solution.py:114
  29.0 5.8 %all-to-all-done.1 = f32[16,1,400]{2,1,0:T(1,128)S(1)} async-done(((f32[16,1,400]{2,1,0:T(1,128)}), f32[16,1,400]{2,1,0:T(1,128)S(1)}, u32[]{:S(2)}, u32[]{:S(2)}) %all-to-all-start.1) | async-done | bytes 25632 | tf_op jit(solution)/shard_map/all_to_all | solution.py:114
  35.6 1.3 fusion.55
  37.2 4.4 %multiply_convert_fusion = (bf16[632,512]{1,0:T(8,128)(2,1)S(1)}, f32[632,512]{1,0:T(8,128)}) fusion(f32[632,512]{1,0:T(8,128)S(1)} %get-tuple-element.47, f32[512]{0:T(512)S(1)} %copy-done.6, f32[512]{0:T(512)S(1)} %copy-done.2, f32[632]{0:T(1024)S(1)} %fusion.26, f32[632]{0:T(1024)S(1)} %broadcast_multiply_fusion), kind=kLoop, calls=%fused_computation.10 | loop fusion | flops 22327296 | bytes 3244992 | tf_op jit(solution)/shard_map/convert_element_type | solution.py:147
  42.2 1.2 fusion.52
  44.1 2.2 fusion.56
  46.5 1.7 fusion.48
  50.7 2.2 convolution_convert_fusion
  53.2 23.4 %reduce-scatter.2.cloned.1.call-done = bf16[768,512]{1,0:T(8,128)(2,1)} async-done(((bf16[1536,512]{1,0:T(8,128)(2,1)}), bf16[768,512]{1,0:T(8,128)(2,1)}) %reduce-scatter.2.cloned.1.call-update) | async-done | bytes 786448 | tf_op jit(solution)/shard_map/reduce_scatter | solution.py:166
  76.5 2.5 %all_gather.17 = f32[768,512]{1,0:T(8,128)} convert(bf16[768,512]{1,0:T(8,128)(2,1)} %reduce-scatter.2.cloned.1.call-done) | non-fusion elementwise | flops 393216 | bytes 2359296 | tf_op jit(solution)/shard_map/all_gather | solution.py:174
  79.1 2.3 %fusion.45 = f32[312,1536]{1,0:T(8,128)S(1)} fusion(bf16[1536,512]{1,0:T(8,128)(2,1)} %all-gather.4.cloned.1.call-done, f32[312,512]{1,0:T(8,128)} %copy-done.1, f32[312]{0:T(512)S(1)} %negate_multiply_fusion.3), kind=kOutput, calls=%fused_computation.115 | convolution fusion | flops 491053056 | bytes 4130016 | tf_op jit(solution)/shard_map/dot_general | solution.py:175
  81.4 2.7 %reshape.197 = f32[8,39,3,512]{3,2,1,0:T(4,128)} reshape(f32[312,1536]{1,0:T(8,128)S(1)} %fusion.45) | data formatting | bytes 3833856 | tf_op jit(solution)/shard_map/reshape | solution.py:48
  84.2 6.1 %fusion.51 = (f32[8,39,1,512]{3,2,1,0:T(1,128)S(1)}, f32[8,39,1,512]{3,2,1,0:T(1,128)S(1)}, f32[8,39,1,512]{3,2,1,0:T(1,128)S(1)}) fusion(f32[8,39,3,512]{3,2,1,0:T(4,128)} %reshape.197), kind=kLoop, calls=%fused_computation.119 | loop fusion | bytes 3833856 | tf_op jit(solution)/shard_map/slice | solution.py:50
  91.7 1.2 reshape.199
  93.0 2.9 %multiply_reduce_fusion = (f32[512]{0:T(512)S(1)}, f32[632]{0:T(1024)S(1)}, f32[512]{0:T(512)S(1)}, f32[632,512]{1,0:T(8,128)S(1)}) fusion(f32[632,512]{1,0:T(8,128)S(1)} %get-tuple-element.47, f32[632]{0:T(1024)S(1)} %fusion.26, f32[632]{0:T(1024)S(1)} %broadcast_multiply_fusion, f32[512]{0:T(512)S(1)} %copy-done.2, f32[632,512]{1,0:T(8,128)} %reshape.199, ...), kind=kLoop, calls=%fused_computation.5 | loop fusion | flops 7440776 | bytes 5193120 | tf_op jit(solution)/shard_map/transpose(jvp())/reduce_sum | solution.py:13
  96.6 1.3 convert_reduce_fusion
  98.7 42.9 %all-reduce.4 = (f32[]{:T(128)}, f32[]{:T(128)}, f32[10,512]{1,0:T(8,128)}, f32[512]{0:T(512)}, f32[512]{0:T(512)}, /*index=5*/f32[512]{0:T(512)}, f32[512]{0:T(512)}) all-reduce(f32[]{:T(128)} %get-tuple-element.15, f32[]{:T(128)} %get-tuple-element.14, f32[10,512]{1,0:T(8,128)S(1)} %fusion.1, ...), channel_id=1, replica_groups=mesh['dp'=16,'fsdp'=2] {'dp','fsdp'}, use_global_device_ids=true, to_apply=%region_9.10 | all-reduce | flops 7170 | bytes 57360 | tf_op jit(solution)/shard_map/psum | solution.py:183
  142.8 66.0 %all-gather.6.cloned.1.call-done = f32[12288,512]{1,0:T(8,128)} async-done(((f32[768,512]{1,0:T(8,128)}), f32[12288,512]{1,0:T(8,128)}) %all-gather.6.cloned.1.call-update) | async-done | bytes 25165840 | tf_op jit(solution)/shard_map/all_gather | solution.py:174
  208.8 10.9 %reduce_sum.188 = f32[768,512]{1,0:T(8,128)} reduce(f32[16,768,512]{2,1,0:T(8,128)} %bitcast.60, f32[]{:T(128)} %constant.48.clone.1), dimensions={0}, to_apply=%region_16.17 | reduce | flops 5898240 | bytes 26738692 | tf_op jit(solution)/shard_map/reduce_sum | solution.py:174
  (75 shorter events, 11.6 us)
Async XLA Ops:
  7.2 28.4 %copy-start = (f32[10,512]{1,0:T(8,128)S(1)}, f32[10,512]{1,0:T(8,128)}, u32[]{:S(2)}) copy-start(f32[10,512]{1,0:T(8,128)} %param.14) | copy-start | bytes 61444
  7.2 36.9 %all-gather.4.cloned.1.call-start = ((), (), s32[]{:S(2)}) async-start(), calls=%async_computation.3 | async-start | bytes 2359296 | tf_op jit(solution)/shard_map/all_gather | solution.py:152
  11.0 13.8 %all-to-all-start = ((f32[16,1,1]{2,1,0:T(1,128)}), f32[16,1,1]{2,1,0:T(1,128)S(1)}, u32[]{:S(2)}, u32[]{:S(2)}) async-start(f32[16,1,1]{2,1,0:T(1,128)} %bitcast.22), calls=%async_computation | async-start | bytes 16384 | tf_op jit(solution)/shard_map/all_to_all | solution.py:121
  24.8 10.1 %all-to-all-start.1 = ((f32[16,1,400]{2,1,0:T(1,128)}), f32[16,1,400]{2,1,0:T(1,128)S(1)}, u32[]{:S(2)}, u32[]{:S(2)}) async-start(f32[16,1,400]{2,1,0:T(1,128)} %copy.79), calls=%async_computation.1 | async-start | bytes 65536 | tf_op jit(solution)/shard_map/all_to_all | solution.py:114
  28.3 48.3 %reduce-scatter.2.cloned.1.call-start = ((), (), s32[]{:S(2)}) async-start(), calls=%async_computation.4 | async-start | bytes 2359296 | tf_op jit(solution)/shard_map/reduce_scatter | solution.py:166
  35.6 1.6 copy-start.2
  35.6 1.6 copy-start.6
  44.0 2.5 %copy-start.3 = (f32[512]{0:T(512)S(1)}, f32[512]{0:T(512)}, u32[]{:S(2)}) copy-start(f32[512]{0:T(512)} %param.18) | copy-start | bytes 6148
  44.0 2.5 %copy-start.5 = (f32[512]{0:T(512)S(1)}, f32[512]{0:T(512)}, u32[]{:S(2)}) copy-start(f32[512]{0:T(512)} %param.19) | copy-start | bytes 6148
  49.9 0.8 copy-start.1
  52.9 155.9 %all-gather.6.cloned.1.call-start = ((), (), s32[]{:S(2)}) async-start(), calls=%async_computation.5 | async-start | bytes 26738688 | tf_op jit(solution)/shard_map/all_gather | solution.py:174
  95.9 0.7 copy-start.4
Sparse Core Ops, SparseCore 0:
  9.5 29.9 all-gather.3
  53.1 23.4 reduce-scatter.1
  79.2 129.6 all-gather.5
